TPU v7x, 32 devices: a whole 2x2x4 slice. The times are simulated.
32 devices in a mesh: expert: 8 (over z, x), dp: 4 (over y, core).
Axes of the slice: x: 2, y: 2, z: 4, core: 2. Of those that a mesh axis runs over, the one named last changes fastest.
Arguments:
- tokens: bfloat16 [1024, 7168], P('expert'), may hold values from -6 to 6
- routes: int32 [1024, 2], P('expert'), may hold values from 0 to 7, all different within a row; in each aligned block of 128 rows (0 to 127, 128 to 255, ...) at most 96 rows name the same one
- route_gates: bfloat16 [1024, 2], P('expert'), may hold values from 0.049804688 to 1
- cotangent: bfloat16 [1024, 7168], P('expert'), may hold values from -6 to 6
- weight_gate: bfloat16 [8, 7168, 1024], P('expert', None, 'dp'), may hold values from -0.0625 to 0.0625
- weight_up: bfloat16 [8, 7168, 1024], P('expert', None, 'dp'), may hold values from -0.0625 to 0.0625
- weight_down: bfloat16 [8, 1024, 7168], P('expert', 'dp'), may hold values from -0.1875 to 0.1875
Outputs:
- grad_tokens: bfloat16 [1024, 7168], P('expert', 'dp')
- grad_gate: bfloat16 [8, 7168, 1024], P('expert', None, 'dp')
- grad_up: bfloat16 [8, 7168, 1024], P('expert', None, 'dp')
- grad_down: bfloat16 [8, 1024, 7168], P('expert', 'dp')
Inputs may be any that keep to these rules, and one draw needn't show every extreme that they name: `routes`: within each aligned block of 128 rows (the tokens of one index of the expert axis) every row names 2 different experts and no expert is named by more than 96 rows; in every draw some block names some expert exactly 96 times.
All inputs are finite; a program needn't handle non-finite values.
Results may differ from a plain program's by a relative error of at most 0.011.
Values may be sent and summed in bfloat16 or wider, within the bound.
A program may use at most 192 MiB of HBM per device.

v0:
```python
import jax
import jax.numpy as jnp
from jax import lax
from jax.sharding import PartitionSpec as P


def slot_layout(routes, experts, capacity):
    flat_routes = routes.reshape(-1)
    onehot = (flat_routes[:, None] == jnp.arange(experts, dtype=jnp.int32)[None, :]).astype(
        jnp.int32
    )
    before = jnp.cumsum(onehot, axis=0) - onehot
    position = jnp.sum(before * onehot, axis=1)
    slot_index = flat_routes * capacity + position
    total_slots = flat_routes.shape[0]
    owners = (
        jnp.full((experts * capacity,), total_slots, dtype=jnp.int32)
        .at[slot_index]
        .set(jnp.arange(total_slots, dtype=jnp.int32))
    )
    return (slot_index, owners)


def pad_rows(source_array, owners, top_count):
    extended = jnp.concatenate(
        [source_array, jnp.zeros((1,) + source_array.shape[1:], source_array.dtype)], 0
    )
    return extended[owners // top_count]


def per_device(tokens, routes, route_gates, cotangent, weight_gate, weight_up, weight_down):
    members = lax.axis_size("expert")
    groups = lax.axis_size("dp")
    local_experts = weight_gate.shape[0]
    experts = members * local_experts
    token_rows = routes.shape[0]
    top_count = routes.shape[1]
    width = tokens.shape[1]
    quarter = width // groups
    capacity = 3 * token_rows * top_count // experts
    slot_index, owners = slot_layout(routes, experts, capacity)
    gate_flat = jnp.concatenate([route_gates.reshape(-1), jnp.zeros((1,), route_gates.dtype)], 0)
    gate_send = gate_flat[owners].reshape(experts, capacity)
    token_send = pad_rows(tokens, owners, top_count).reshape(experts, capacity, width)
    back_send = pad_rows(cotangent, owners, top_count).reshape(experts, capacity, width)
    token_arrived, back_arrived, gate_arrived = (
        lax.all_to_all(token_send, "expert", split_axis=0, concat_axis=1, tiled=True),
        lax.all_to_all(back_send, "expert", split_axis=0, concat_axis=1, tiled=True),
        lax.all_to_all(gate_send, "expert", split_axis=0, concat_axis=1, tiled=True),
    )
    scale = gate_arrived.astype(jnp.float32)[:, :, None]
    pre_gate = jnp.einsum(
        "erd,edf->erf", token_arrived, weight_gate, preferred_element_type=jnp.float32
    )
    pre_up = jnp.einsum(
        "erd,edf->erf", token_arrived, weight_up, preferred_element_type=jnp.float32
    )
    sigma = jax.nn.sigmoid(pre_gate)
    activated = pre_gate * sigma
    scaled_hidden = (scale * activated * pre_up).astype(jnp.bfloat16)
    back_hidden = scale * jnp.einsum(
        "erd,efd->erf", back_arrived, weight_down, preferred_element_type=jnp.float32
    )
    back_up = (back_hidden * activated).astype(jnp.bfloat16)
    back_gate = (back_hidden * pre_up * sigma * (1.0 + pre_gate * (1.0 - sigma))).astype(
        jnp.bfloat16
    )
    grad_gate = jnp.einsum(
        "erd,erf->edf", token_arrived, back_gate, preferred_element_type=jnp.float32
    ).astype(jnp.bfloat16)
    grad_up = jnp.einsum(
        "erd,erf->edf", token_arrived, back_up, preferred_element_type=jnp.float32
    ).astype(jnp.bfloat16)
    grad_down = jnp.einsum(
        "erf,erd->efd", scaled_hidden, back_arrived, preferred_element_type=jnp.float32
    ).astype(jnp.bfloat16)
    up_term = jnp.einsum("edf,erf->der", weight_up, back_up, preferred_element_type=jnp.float32)
    gate_term = jnp.einsum(
        "edf,erf->der", weight_gate, back_gate, preferred_element_type=jnp.float32
    )
    slot_back = lax.psum_scatter(
        (up_term + gate_term).astype(jnp.bfloat16), "dp", scatter_dimension=0, tiled=True
    )
    returned = lax.all_to_all(slot_back, "expert", split_axis=2, concat_axis=1, tiled=True)
    flat_back = returned.reshape(quarter, experts * capacity)
    picked = (
        jnp.take(flat_back, slot_index, axis=1)
        .astype(jnp.float32)
        .reshape(quarter, token_rows, top_count)
    )
    grad_tokens = jnp.sum(picked, axis=2).T.astype(jnp.bfloat16)
    return (grad_tokens, grad_gate, grad_up, grad_down)


def solution(mesh):
    placed = (
        P("expert", None),
        P("expert", None),
        P("expert", None),
        P("expert", None),
        P("expert", None, "dp"),
        P("expert", None, "dp"),
        P("expert", "dp", None),
    )
    return jax.shard_map(
        per_device,
        mesh=mesh,
        in_specs=placed,
        out_specs=(
            P("expert", "dp"),
            P("expert", None, "dp"),
            P("expert", None, "dp"),
            P("expert", "dp", None),
        ),
        check_vma=False,
    )
```

profile of v0, /device:TPU:0, one launch (start us, length us, event | category | flops | bytes accessed | tf_op | source)
XLA Modules:
  0.0 770.3 jit_solution(8576594936999472891)
XLA Ops:
  11.1 1.4 scatter_custom_fusion
  12.5 5.0 gather_fusion
  18.2 7.3 all-to-all-start
  25.5 1.7 concatenate.11
  27.2 9.4 %gather_fusion.2 = bf16[768,7168]{1,0:T(8,128)(2,1)} fusion(bf16[129,7168]{1,0:T(8,128)(2,1)S(1)} %concatenate.11, s32[1024]{0:T(1024)S(1)} %get-tuple-element.9), kind=kCustom, calls=%fused_computation.2 | custom fusion | bytes 22023168 | tf_op jit(solution)/shard_map/gather | solution.py:28
  36.6 6.0 all-to-all-start.2
  42.6 1.7 concatenate.10
  44.3 9.5 %gather_fusion.1 = bf16[768,7168]{1,0:T(8,128)(2,1)} fusion(bf16[129,7168]{1,0:T(8,128)(2,1)S(1)} %concatenate.10, s32[1024]{0:T(1024)S(1)} %get-tuple-element.9), kind=kCustom, calls=%fused_computation.1 | custom fusion | bytes 22023168 | tf_op jit(solution)/shard_map/gather | solution.py:28
  53.7 227.6 %all-to-all-done.2 = bf16[8,96,7168]{2,1,0:T(8,128)(2,1)} async-done(((bf16[8,96,7168]{2,1,0:T(8,128)(2,1)}), bf16[8,96,7168]{2,1,0:T(8,128)(2,1)}, u32[]{:S(2)}, u32[]{:S(2)}) %all-to-all-start.2) | async-done | bytes 11010080 | tf_op jit(solution)/shard_map/all_to_all | solution.py:47
  281.4 5.2 all-to-all-start.1
  287.0 6.9 fusion.4
  293.9 230.6 %all-to-all-done.1 = bf16[8,96,7168]{2,1,0:T(8,128)(2,1)} async-done(((bf16[8,96,7168]{2,1,0:T(8,128)(2,1)}), bf16[8,96,7168]{2,1,0:T(8,128)(2,1)}, u32[]{:S(2)}, u32[]{:S(2)}) %all-to-all-start.1) | async-done | bytes 11010080 | tf_op jit(solution)/shard_map/all_to_all | solution.py:48
  524.5 7.1 fusion.13
  531.6 8.3 %multiply_convert_fusion.1 = (bf16[768,256]{1,0:T(8,128)(2,1)S(1)}, bf16[768,256]{1,0:T(8,128)(2,1)S(1)}, f32[768,256]{1,0:T(8,128)}) fusion(f32[768,256]{1,0:T(8,128)S(1)} %fusion.13, f32[768,256]{1,0:T(8,128)S(1)} %fusion.4, bf16[768,7168]{1,0:T(8,128)(2,1)} %bitcast.8, bf16[1,7168,256]{2,1,0:T(8,128)(2,1)S(1)} %copy-done.1), kind=kOutput, calls=%fused_computation.27 | convolution fusion | flops 2821128192 | bytes 17825792 | tf_op jit(solution)/shard_map/erd,edf->erf/dot_general | solution.py:52
  540.0 9.1 %fusion.6 = f32[768,7168]{1,0:T(8,128)} fusion(bf16[768,256]{1,0:T(8,128)(2,1)S(1)} %get-tuple-element.5, bf16[1,7168,256]{2,1,0:T(8,128)(2,1)S(1)} %copy-done), kind=kOutput, calls=%fused_computation.15 | convolution fusion | flops 2818572288 | bytes 26083328 | tf_op jit(solution)/shard_map/edf,erf->der/dot_general | solution.py:77
  549.0 12.8 %fusion = bf16[7168,1,768]{0,2,1:T(8,128)(2,1)} fusion(f32[768,7168]{1,0:T(8,128)} %fusion.6, bf16[768,256]{1,0:T(8,128)(2,1)S(1)} %get-tuple-element.4, bf16[1,7168,256]{2,1,0:T(8,128)(2,1)S(1)} %copy-done.1), kind=kOutput, calls=%fused_computation.6 | convolution fusion | flops 2829582336 | bytes 37093376 | tf_op jit(solution)/shard_map/edf,erf->der/dot_general | solution.py:78
  561.9 88.4 %reduce-scatter.2.cloned.1.call-done = bf16[1792,1,768]{0,2,1:T(8,128)(2,1)} async-done(((bf16[7168,1,768]{0,2,1:T(8,128)(2,1)}), bf16[1792,1,768]{0,2,1:T(8,128)(2,1)}) %reduce-scatter.2.cloned.1.call-update) | async-done | bytes 2752528 | tf_op jit(solution)/shard_map/reduce_scatter | solution.py:81
  650.3 8.4 %copy.44 = bf16[1792,1,768]{0,1,2:T(2,128)(2,1)} copy(bf16[1792,1,768]{0,2,1:T(8,128)(2,1)} %reduce-scatter.2.cloned.1.call-done) | data formatting | bytes 5505024 | tf_op jit(solution)/shard_map/reduce_scatter | solution.py:81
  659.2 17.0 %reduce.7 = bf16[768,1792]{1,0:T(8,128)(2,1)S(1)} reduce(bf16[768,1,1792]{2,1,0:T(2,128)(2,1)} %bitcast.67, bf16[]{:T(256)} %broadcast.118), dimensions={1}, to_apply=%bitcast.62.reduce_sub_computation | reduce | bytes 5505026
  676.3 3.5 reshape.245
  679.7 5.7 all-to-all-start.3
  686.2 0.9 copy.32
  687.6 1.4 copy.33
  689.0 9.5 %fusion.3 = bf16[1,256,7168]{2,1,0:T(8,128)(2,1)} fusion(bf16[768,7168]{1,0:T(8,128)(2,1)} %bitcast.5, f32[768,256]{1,0:T(8,128)S(1)} %fusion.4, f32[768]{0:T(1024)S(1)} %reshape.191, f32[768,256]{1,0:T(8,128)} %get-tuple-element.8), kind=kOutput, calls=%fused_computation.12 | convolution fusion | flops 2821783552 | bytes 16256000 | tf_op jit(solution)/shard_map/erf,erd->efd/dot_general | solution.py:74
  698.5 9.1 %fusion.1 = bf16[1,7168,256]{2,1,0:T(8,128)(2,1)} fusion(bf16[768,7168]{1,0:T(8,128)(2,1)} %bitcast.8, bf16[768,256]{1,0:T(8,128)(2,1)S(1)} %copy-done.3), kind=kOutput, calls=%fused_computation.10 | convolution fusion | flops 2820407296 | bytes 15073280 | tf_op jit(solution)/shard_map/erd,erf->edf/dot_general | solution.py:68
  707.6 9.1 %fusion.2 = bf16[1,7168,256]{2,1,0:T(8,128)(2,1)} fusion(bf16[768,7168]{1,0:T(8,128)(2,1)} %bitcast.8, bf16[768,256]{1,0:T(8,128)(2,1)S(1)} %copy-done.5), kind=kOutput, calls=%fused_computation.11 | convolution fusion | flops 2820407296 | bytes 15073280 | tf_op jit(solution)/shard_map/erd,erf->edf/dot_general | solution.py:71
  716.7 31.0 %all-to-all-done.3 = bf16[8,2,86016]{2,1,0:T(2,128)(2,1)S(1)} async-done(((bf16[8,2,86016]{2,1,0:T(2,128)(2,1)}), bf16[8,2,86016]{2,1,0:T(2,128)(2,1)S(1)}, u32[]{:S(2)}, u32[]{:S(2)}) %all-to-all-start.3) | async-done | bytes 2752544 | tf_op jit(solution)/shard_map/all_to_all | solution.py:84
  747.7 4.9 reshape.246
  752.6 3.0 copy.43
  755.6 2.3 gather_fusion.3
  757.9 2.5 gather.19
  760.4 2.8 fusion.16
  (45 shorter events, 6.9 us)
Async XLA Ops:
  18.2 18.3 %all-to-all-start = ((bf16[8,1,96]{2,1,0:T(2,128)(2,1)}), bf16[8,1,96]{2,1,0:T(2,128)(2,1)S(1)}, u32[]{:S(2)}, u32[]{:S(2)}) async-start(bf16[8,1,96]{2,1,0:T(2,128)(2,1)} %all_to_all.16), calls=%async_computation | async-start | bytes 8192 | tf_op jit(solution)/shard_map/all_to_all | solution.py:49
  36.6 244.8 %all-to-all-start.2 = ((bf16[8,96,7168]{2,1,0:T(8,128)(2,1)}), bf16[8,96,7168]{2,1,0:T(8,128)(2,1)}, u32[]{:S(2)}, u32[]{:S(2)}) async-start(bf16[8,96,7168]{2,1,0:T(8,128)(2,1)} %bitcast.65), calls=%async_computation.2 | async-start | bytes 22020096 | tf_op jit(solution)/shard_map/all_to_all | solution.py:47
  281.4 243.2 %all-to-all-start.1 = ((bf16[8,96,7168]{2,1,0:T(8,128)(2,1)}), bf16[8,96,7168]{2,1,0:T(8,128)(2,1)}, u32[]{:S(2)}, u32[]{:S(2)}) async-start(bf16[8,96,7168]{2,1,0:T(8,128)(2,1)} %bitcast.64), calls=%async_computation.1 | async-start | bytes 22020096 | tf_op jit(solution)/shard_map/all_to_all | solution.py:48
  286.6 363.7 %reduce-scatter.2.cloned.1.call-start = ((), (), s32[]{:S(2)}) async-start(), calls=%async_computation.5 | async-start | bytes 13762560 | tf_op jit(solution)/shard_map/reduce_scatter | solution.py:81
  524.5 7.1 copy-start.1
  531.6 8.3 %copy-start = (bf16[1,7168,256]{2,1,0:T(8,128)(2,1)S(1)}, bf16[1,7168,256]{2,1,0:T(8,128)(2,1)}, u32[]{:S(2)}) copy-start(bf16[1,7168,256]{2,1,0:T(8,128)(2,1)} %param.12) | copy-start | bytes 11010052
  540.0 9.1 %copy-start.4 = (bf16[768,256]{1,0:T(8,128)(2,1)}, bf16[768,256]{1,0:T(8,128)(2,1)S(1)}, u32[]{:S(2)}) copy-start(bf16[768,256]{1,0:T(8,128)(2,1)S(1)} %get-tuple-element.5) | copy-start | bytes 1179652
  540.0 9.1 %copy-start.2 = (bf16[768,256]{1,0:T(8,128)(2,1)}, bf16[768,256]{1,0:T(8,128)(2,1)S(1)}, u32[]{:S(2)}) copy-start(bf16[768,256]{1,0:T(8,128)(2,1)S(1)} %get-tuple-element.4) | copy-start | bytes 1179652
  676.2 10.9 %copy-start.7 = (s32[128,2]{0,1:T(2,128)S(1)}, s32[128,2]{0,1:T(2,128)}, u32[]{:S(2)}) copy-start(s32[128,2]{0,1:T(2,128)} %param.8) | copy-start | bytes 3076
  679.7 68.0 %all-to-all-start.3 = ((bf16[8,2,86016]{2,1,0:T(2,128)(2,1)}), bf16[8,2,86016]{2,1,0:T(2,128)(2,1)S(1)}, u32[]{:S(2)}, u32[]{:S(2)}) async-start(bf16[8,2,86016]{2,1,0:T(2,128)(2,1)} %reshape.245), calls=%async_computation.4 | async-start | bytes 5505024 | tf_op jit(solution)/shard_map/all_to_all | solution.py:84
  689.0 9.5 %copy-start.3 = (bf16[768,256]{1,0:T(8,128)(2,1)S(1)}, bf16[768,256]{1,0:T(8,128)(2,1)}, u32[]{:S(2)}) copy-start(bf16[768,256]{1,0:T(8,128)(2,1)} %copy-done.2) | copy-start | bytes 1179652
  698.5 9.1 %copy-start.5 = (bf16[768,256]{1,0:T(8,128)(2,1)S(1)}, bf16[768,256]{1,0:T(8,128)(2,1)}, u32[]{:S(2)}) copy-start(bf16[768,256]{1,0:T(8,128)(2,1)} %copy-done.4) | copy-start | bytes 1179652
  752.6 7.8 %copy-start.6 = (pred[128,2]{1,0:T(8,128)(4,1)S(1)}, pred[128,2]{1,0:T(8,128)(4,1)}, u32[]{:S(2)}) copy-start(pred[128,2]{1,0:T(8,128)(4,1)} %copy.33) | copy-start | bytes 772
Sparse Core Ops, SparseCore 0:
  562.0 88.2 reduce-scatter.1
where the time goes:
time: 776 us; the launch traced here: 770 us
  waiting for transfers between devices  578 us (74%)
  matrix products  71.9 us (9%)
  local copies, waits for them, and re-layouts  60 us (8%)
  starting transfers between devices  24.5 us (3%)
  other arithmetic  21.8 us (3%)
  between operations  14.5 us (2%)
    all_to_all x1, waiting for transfers between devices, per_device(): lax.all_to_all(back_send, 'expert', split_axis=0, concat_axis=1, tiled=True)  231 us
    all_to_all x1, waiting for transfers between devices, per_device(): lax.all_to_all(token_send, 'expert', split_axis=0, concat_axis=1, tiled=T...  228 us
    reduce_scatter x1, waiting for transfers between devices, per_device(): lax.psum_scatter((up_term + gate_term).astype(jnp.bfloat16), 'dp', scatte...  88.4 us
    all_to_all x1, waiting for transfers between devices, per_device(): lax.all_to_all(slot_back, 'expert', split_axis=2, concat_axis=1, tiled=True)  31 us
    gather x2, local copies, waits for them, and re-layouts, pad_rows(): return extended[owners // top_count]  18.9 us
    unnamed x1, other arithmetic  17 us
  transfers between devices with their start and end apart: 5, of which 4 were waited for; matrix products, arithmetic and copies ran while one was open for 8% of the time, Pallas kernels for 0%

commit v1 on v0

--- a/solution.py
+++ b/solution.py
@@ -81,7 +81,12 @@
     slot_back = lax.psum_scatter(
         (up_term + gate_term).astype(jnp.bfloat16), "dp", scatter_dimension=0, tiled=True
     )
-    returned = lax.all_to_all(slot_back, "expert", split_axis=2, concat_axis=1, tiled=True)
+    returned = jnp.concatenate(
+        lax.all_to_all(
+            jnp.stack(jnp.split(slot_back, lax.axis_size("expert"), axis=2)), "expert", 0, 0
+        ),
+        axis=1,
+    )
     flat_back = returned.reshape(quarter, experts * capacity)
     picked = (
         jnp.take(flat_back, slot_index, axis=1)

time: 776 us -> 747 us (0.963)
  other arithmetic: 21.8 us -> 4.82 us
    unnamed x1 -> x0, other arithmetic: 17 us -> none
    reduce_scatter x1 -> x0, local copies, waits for them, and re-layouts: 8.41 us -> none  [per_device(): lax.psum_scatter((up_term + gate_term).astype(jnp.bfloat16), 'dp', scatte...]
where the time goes in v1:
time: 747 us; the launch traced here: 746 us
  waiting for transfers between devices  578 us (77%)
  matrix products  71.4 us (10%)
  local copies, waits for them, and re-layouts  53.4 us (7%)
  starting transfers between devices  24.2 us (3%)
  between operations  14.2 us (2%)
    all_to_all x1, waiting for transfers between devices, per_device(): lax.all_to_all(back_send, 'expert', split_axis=0, concat_axis=1, tiled=True)  231 us
    all_to_all x1, waiting for transfers between devices, per_device(): lax.all_to_all(token_send, 'expert', split_axis=0, concat_axis=1, tiled=T...  228 us
    reduce_scatter x1, waiting for transfers between devices, per_device(): lax.psum_scatter((up_term + gate_term).astype(jnp.bfloat16), 'dp', scatte...  88.4 us
    all_to_all x1, waiting for transfers between devices, per_device(): lax.all_to_all(jnp.stack(jnp.split(slot_back, lax.axis_size('expert'), ax...  31 us
    gather x2, local copies, waits for them, and re-layouts, pad_rows(): return extended[owners // top_count]  18.9 us
  transfers between devices with their start and end apart: 5, of which 4 were waited for; matrix products, arithmetic and copies ran while one was open for 8% of the time, Pallas kernels for 0%

profile of v1, /device:TPU:0, one launch (start us, length us, event | category | flops | bytes accessed | tf_op | source)
XLA Modules:
  0.0 745.9 jit_solution(13824162419636644597)
XLA Ops:
  12.5 5.0 gather_fusion
  18.2 7.3 all-to-all-start
  25.5 1.7 concatenate.11
  27.2 9.4 %gather_fusion.2 = bf16[768,7168]{1,0:T(8,128)(2,1)} fusion(bf16[129,7168]{1,0:T(8,128)(2,1)S(1)} %concatenate.11, s32[1024]{0:T(1024)S(1)} %get-tuple-element.9), kind=kCustom, calls=%fused_computation.2 | custom fusion | bytes 22023168 | tf_op jit(solution)/shard_map/gather | solution.py:28
  36.6 6.0 all-to-all-start.2
  42.6 1.7 concatenate.10
  44.3 9.5 %gather_fusion.1 = bf16[768,7168]{1,0:T(8,128)(2,1)} fusion(bf16[129,7168]{1,0:T(8,128)(2,1)S(1)} %concatenate.10, s32[1024]{0:T(1024)S(1)} %get-tuple-element.9), kind=kCustom, calls=%fused_computation.1 | custom fusion | bytes 22023168 | tf_op jit(solution)/shard_map/gather | solution.py:28
  53.7 227.6 %all-to-all-done.2 = bf16[8,96,7168]{2,1,0:T(8,128)(2,1)} async-done(((bf16[8,96,7168]{2,1,0:T(8,128)(2,1)}), bf16[8,96,7168]{2,1,0:T(8,128)(2,1)}, u32[]{:S(2)}, u32[]{:S(2)}) %all-to-all-start.2) | async-done | bytes 11010080 | tf_op jit(solution)/shard_map/all_to_all | solution.py:47
  281.4 5.2 all-to-all-start.1
  286.9 6.9 fusion.4
  293.8 230.7 %all-to-all-done.1 = bf16[8,96,7168]{2,1,0:T(8,128)(2,1)} async-done(((bf16[8,96,7168]{2,1,0:T(8,128)(2,1)}), bf16[8,96,7168]{2,1,0:T(8,128)(2,1)}, u32[]{:S(2)}, u32[]{:S(2)}) %all-to-all-start.1) | async-done | bytes 11010080 | tf_op jit(solution)/shard_map/all_to_all | solution.py:48
  524.5 7.1 fusion.13
  531.6 8.3 %multiply_convert_fusion.1 = (bf16[768,256]{1,0:T(8,128)(2,1)S(1)}, bf16[768,256]{1,0:T(8,128)(2,1)S(1)}, f32[768,256]{1,0:T(8,128)}) fusion(f32[768,256]{1,0:T(8,128)S(1)} %fusion.13, f32[768,256]{1,0:T(8,128)S(1)} %fusion.4, bf16[768,7168]{1,0:T(8,128)(2,1)} %bitcast.8, bf16[1,7168,256]{2,1,0:T(8,128)(2,1)S(1)} %copy-done.1), kind=kOutput, calls=%fused_computation.26 | convolution fusion | flops 2821128192 | bytes 17825792 | tf_op jit(solution)/shard_map/erd,edf->erf/dot_general | solution.py:52
  540.0 9.0 %fusion.6 = f32[768,7168]{1,0:T(8,128)} fusion(bf16[768,256]{1,0:T(8,128)(2,1)S(1)} %get-tuple-element.5, bf16[1,7168,256]{2,1,0:T(8,128)(2,1)S(1)} %copy-done), kind=kOutput, calls=%fused_computation.15 | convolution fusion | flops 2818572288 | bytes 26083328 | tf_op jit(solution)/shard_map/edf,erf->der/dot_general | solution.py:77
  549.0 12.3 %fusion = bf16[7168,1,768]{0,2,1:T(8,128)(2,1)} fusion(f32[768,7168]{1,0:T(8,128)} %fusion.6, bf16[768,256]{1,0:T(8,128)(2,1)S(1)} %get-tuple-element.4, bf16[1,7168,256]{2,1,0:T(8,128)(2,1)S(1)} %copy-done.1), kind=kOutput, calls=%fused_computation.6 | convolution fusion | flops 2829582336 | bytes 37093376 | tf_op jit(solution)/shard_map/edf,erf->der/dot_general | solution.py:78
  561.4 88.4 %reduce-scatter.2.cloned.1.call-done = bf16[1792,1,768]{0,2,1:T(8,128)(2,1)} async-done(((bf16[7168,1,768]{0,2,1:T(8,128)(2,1)}), bf16[1792,1,768]{0,2,1:T(8,128)(2,1)}) %reduce-scatter.2.cloned.1.call-update) | async-done | bytes 2752528 | tf_op jit(solution)/shard_map/reduce_scatter | solution.py:81
  649.8 1.7 fusion.26
  651.5 1.8 fusion.25
  653.3 1.7 fusion.24
  655.0 1.7 fusion.23
  656.8 1.7 fusion.22
  658.5 1.7 fusion.21
  660.3 1.8 fusion.20
  662.0 1.7 fusion.19
  663.7 5.5 all-to-all-start.3
  672.8 9.5 %fusion.3 = bf16[1,256,7168]{2,1,0:T(8,128)(2,1)} fusion(bf16[768,7168]{1,0:T(8,128)(2,1)} %bitcast.5, f32[768,256]{1,0:T(8,128)S(1)} %fusion.4, f32[768]{0:T(1024)S(1)} %reshape.187, f32[768,256]{1,0:T(8,128)} %get-tuple-element.8), kind=kOutput, calls=%fused_computation.12 | convolution fusion | flops 2821783552 | bytes 16256000 | tf_op jit(solution)/shard_map/erf,erd->efd/dot_general | solution.py:74
  682.3 9.1 %fusion.1 = bf16[1,7168,256]{2,1,0:T(8,128)(2,1)} fusion(bf16[768,7168]{1,0:T(8,128)(2,1)} %bitcast.8, bf16[768,256]{1,0:T(8,128)(2,1)S(1)} %copy-done.3), kind=kOutput, calls=%fused_computation.10 | convolution fusion | flops 2820407296 | bytes 15073280 | tf_op jit(solution)/shard_map/erd,erf->edf/dot_general | solution.py:68
  691.5 9.1 %fusion.2 = bf16[1,7168,256]{2,1,0:T(8,128)(2,1)} fusion(bf16[768,7168]{1,0:T(8,128)(2,1)} %bitcast.8, bf16[768,256]{1,0:T(8,128)(2,1)S(1)} %copy-done.5), kind=kOutput, calls=%fused_computation.11 | convolution fusion | flops 2820407296 | bytes 15073280 | tf_op jit(solution)/shard_map/erd,erf->edf/dot_general | solution.py:71
  700.5 31.0 %all-to-all-done.3 = bf16[8,1792,1,96]{1,3,2,0:T(8,128)(2,1)S(1)} async-done(((bf16[8,1792,1,96]{1,3,2,0:T(8,128)(2,1)}), bf16[8,1792,1,96]{1,3,2,0:T(8,128)(2,1)S(1)}, u32[]{:S(2)}, u32[]{:S(2)}) %all-to-all-start.3) | async-done | bytes 2752544 | tf_op jit(solution)/shard_map/all_to_all | solution.py:85
  731.6 2.3 gather_fusion.3
  733.8 2.3 gather.19
  736.2 2.8 fusion.16
  (47 shorter events, 9.9 us)
Async XLA Ops:
  18.2 18.3 %all-to-all-start = ((bf16[8,1,96]{2,1,0:T(2,128)(2,1)}), bf16[8,1,96]{2,1,0:T(2,128)(2,1)S(1)}, u32[]{:S(2)}, u32[]{:S(2)}) async-start(bf16[8,1,96]{2,1,0:T(2,128)(2,1)} %all_to_all.32), calls=%async_computation | async-start | bytes 8192 | tf_op jit(solution)/shard_map/all_to_all | solution.py:49
  36.6 244.8 %all-to-all-start.2 = ((bf16[8,96,7168]{2,1,0:T(8,128)(2,1)}), bf16[8,96,7168]{2,1,0:T(8,128)(2,1)}, u32[]{:S(2)}, u32[]{:S(2)}) async-start(bf16[8,96,7168]{2,1,0:T(8,128)(2,1)} %bitcast.92), calls=%async_computation.2 | async-start | bytes 22020096 | tf_op jit(solution)/shard_map/all_to_all | solution.py:47
  281.4 243.2 %all-to-all-start.1 = ((bf16[8,96,7168]{2,1,0:T(8,128)(2,1)}), bf16[8,96,7168]{2,1,0:T(8,128)(2,1)}, u32[]{:S(2)}, u32[]{:S(2)}) async-start(bf16[8,96,7168]{2,1,0:T(8,128)(2,1)} %bitcast.91), calls=%async_computation.1 | async-start | bytes 22020096 | tf_op jit(solution)/shard_map/all_to_all | solution.py:48
  286.6 363.2 %reduce-scatter.2.cloned.1.call-start = ((), (), s32[]{:S(2)}) async-start(), calls=%async_computation.5 | async-start | bytes 13762560 | tf_op jit(solution)/shard_map/reduce_scatter | solution.py:81
  524.5 7.1 copy-start.1
  531.6 8.3 %copy-start = (bf16[1,7168,256]{2,1,0:T(8,128)(2,1)S(1)}, bf16[1,7168,256]{2,1,0:T(8,128)(2,1)}, u32[]{:S(2)}) copy-start(bf16[1,7168,256]{2,1,0:T(8,128)(2,1)} %param.12) | copy-start | bytes 11010052
  540.0 9.1 %copy-start.4 = (bf16[768,256]{1,0:T(8,128)(2,1)}, bf16[768,256]{1,0:T(8,128)(2,1)S(1)}, u32[]{:S(2)}) copy-start(bf16[768,256]{1,0:T(8,128)(2,1)S(1)} %get-tuple-element.5) | copy-start | bytes 1179652
  540.0 9.1 %copy-start.2 = (bf16[768,256]{1,0:T(8,128)(2,1)}, bf16[768,256]{1,0:T(8,128)(2,1)S(1)}, u32[]{:S(2)}) copy-start(bf16[768,256]{1,0:T(8,128)(2,1)S(1)} %get-tuple-element.4) | copy-start | bytes 1179652
  660.2 10.7 %copy-start.7 = (s32[128,2]{0,1:T(2,128)S(1)}, s32[128,2]{0,1:T(2,128)}, u32[]{:S(2)}) copy-start(s32[128,2]{0,1:T(2,128)} %param.8) | copy-start | bytes 3076
  663.7 67.8 %all-to-all-start.3 = ((bf16[8,1792,1,96]{1,3,2,0:T(8,128)(2,1)}), bf16[8,1792,1,96]{1,3,2,0:T(8,128)(2,1)S(1)}, u32[]{:S(2)}, u32[]{:S(2)}) async-start(bf16[8,1792,1,96]{1,3,2,0:T(8,128)(2,1)} %fusion.19), calls=%async_computation.4 | async-start | bytes 5505024 | tf_op jit(solution)/shard_map/all_to_all | solution.py:85
  672.8 9.5 %copy-start.3 = (bf16[768,256]{1,0:T(8,128)(2,1)S(1)}, bf16[768,256]{1,0:T(8,128)(2,1)}, u32[]{:S(2)}) copy-start(bf16[768,256]{1,0:T(8,128)(2,1)} %copy-done.2) | copy-start | bytes 1179652
  682.3 9.1 %copy-start.5 = (bf16[768,256]{1,0:T(8,128)(2,1)S(1)}, bf16[768,256]{1,0:T(8,128)(2,1)}, u32[]{:S(2)}) copy-start(bf16[768,256]{1,0:T(8,128)(2,1)} %copy-done.4) | copy-start | bytes 1179652
  731.6 4.6 copy-start.6
Sparse Core Ops, SparseCore 0:
  561.5 88.2 reduce-scatter.1
